TPU v7x, 512 devices: a whole 4x8x8 slice. The times are simulated.
512 devices in a mesh: ctx: 32 (over x_hi, y, core), batch: 16 (over z, x_lo).
Axes of the slice: x: 4 (x_hi: 2, x_lo: 2; x = x_hi * 2 + x_lo), y: 8, z: 8, core: 2. Of those that a mesh axis runs over, the one named last changes fastest.
Arguments:
- seq_in: bfloat16 [16, 4096, 512], P('batch', 'ctx'), may hold values from -6 to 6
- w_in: bfloat16 [512, 2048], replicated, may hold values from -0.25 to 0.25
- w_out: bfloat16 [512, 512], replicated, may hold values from -0.25 to 0.25
- pos_emb: bfloat16 [16, 4096, 512], P('batch', 'ctx'), may hold values from -0.29882812 to 0.29882812
- pos_ids: int32 [16, 4096], P('batch', 'ctx'), may hold values from 0 to 3999999, as said below
- neg_emb: bfloat16 [128, 512], P('batch'), may hold values from -0.29882812 to 0.29882812
- neg_ids: int32 [128], P('batch'), may hold values from 0 to 3999999
- neg_counts: int32 [128], P('batch'), may hold values from 1000 to 99999
Outputs:
- loss: float32 [16, 4096], P('batch', 'ctx')
- d_seq: bfloat16 [16, 4096, 512], P('batch', 'ctx')
- d_neg: float32 [128, 512], P('batch')
Inputs may be any that keep to these rules, and one draw needn't show every extreme that they name: `pos_ids`: item ids; many positions name the item of one of the sampled negatives.
All inputs are finite; a program needn't handle non-finite values.
Results may differ from a plain program's by a relative error of at most 0.008.
Values may be sent and summed in bfloat16 or wider, within the bound.
A program may use at most 128 MiB of HBM per device.

v0:
```python
import math
import jax
import jax.numpy as jnp
from jax import lax
from jax.sharding import PartitionSpec as P

HEADS = 8
HEAD = 64
D = 512
SOFTMAX_TEMPER = 0.05


def silu_slope(scores):
    sigma = jax.nn.sigmoid(scores)
    return sigma * (1.0 + scores * (1.0 - sigma))


def split_heads(matrix):
    return matrix.reshape(matrix.shape[0], HEADS, HEAD)


def shards(seq_in, w_in, w_out, pos_emb, pos_ids, neg_emb, neg_ids, neg_counts):
    tokens = seq_in.shape[1]
    score_scale = HEAD ** (-0.5)
    offset = lax.axis_index("ctx") * tokens
    row_pos = offset + lax.iota(jnp.int32, tokens)
    neg_float = neg_emb.astype(jnp.float32)
    neg_scale = lax.rsqrt(jnp.sum(neg_float * neg_float, axis=1, keepdims=True) + 1e-06)
    neg_unit = neg_float * neg_scale
    every_unit_vector, all_ids, all_counts = (
        lax.all_gather(neg_unit.astype(jnp.bfloat16), "batch", axis=0, tiled=True),
        lax.all_gather(neg_ids, "batch", axis=0, tiled=True),
        lax.all_gather(neg_counts, "batch", axis=0, tiled=True),
    )
    count_float = all_counts.astype(jnp.float32)
    log_sample_share = jnp.log(all_counts.shape[0] * count_float / jnp.sum(count_float))
    seq_x = seq_in[0]
    pre_act = jnp.dot(seq_x, w_in, preferred_element_type=jnp.float32)
    proj = jax.nn.silu(pre_act).astype(jnp.bfloat16)
    gate_u = proj[:, :D].astype(jnp.float32)
    value_rows = proj[:, D : 2 * D]
    query_rows = proj[:, 2 * D : 3 * D]
    key_rows = proj[:, 3 * D :]
    all_values, all_keys = (
        lax.all_gather(value_rows, "ctx", axis=0, tiled=True),
        lax.all_gather(key_rows, "ctx", axis=0, tiled=True),
    )
    length = all_keys.shape[0]
    block_rows = math.gcd(length, 512)
    heads_keys = split_heads(all_keys)
    heads_values = split_heads(all_values)
    local_q = split_heads(query_rows)
    local_k = split_heads(key_rows)
    local_v = split_heads(value_rows)
    empty = jnp.zeros((tokens, HEADS, HEAD), jnp.float32)

    def forward_step(index, carry):
        start = index * block_rows
        keys_blk = lax.dynamic_slice_in_dim(heads_keys, start, block_rows, 0)
        values_blk = lax.dynamic_slice_in_dim(heads_values, start, block_rows, 0)
        scores = (
            jnp.einsum("ihe,jhe->hij", local_q, keys_blk, preferred_element_type=jnp.float32)
            * score_scale
        )
        allowed = ((start + lax.iota(jnp.int32, block_rows))[None, :] <= row_pos[:, None])[None]
        weights = jnp.where(allowed, jax.nn.silu(scores), 0.0).astype(jnp.bfloat16)
        return carry + jnp.einsum(
            "hij,jhe->ihe", weights, values_blk, preferred_element_type=jnp.float32
        )

    mixed = lax.fori_loop(0, length // block_rows, forward_step, empty).reshape(tokens, D)
    centred = mixed - jnp.mean(mixed, axis=1, keepdims=True)
    inv_std = lax.rsqrt(jnp.mean(centred * centred, axis=1, keepdims=True) + 1e-05)
    normed = centred * inv_std
    gated = (normed * gate_u).astype(jnp.bfloat16)
    outputs = seq_x.astype(jnp.float32) + jnp.dot(gated, w_out, preferred_element_type=jnp.float32)
    out_scale = lax.rsqrt(jnp.sum(outputs * outputs, axis=1, keepdims=True) + 1e-06)
    user_vector = outputs * out_scale
    user_rounded = user_vector.astype(jnp.bfloat16)
    pos_float = pos_emb[0].astype(jnp.float32)
    positive_unit = pos_float * lax.rsqrt(
        jnp.sum(pos_float * pos_float, axis=1, keepdims=True) + 1e-06
    )
    positive_item = jnp.sum(user_vector * positive_unit, axis=1) / SOFTMAX_TEMPER
    score_logits = (
        jnp.einsum("id,nd->in", user_rounded, every_unit_vector, preferred_element_type=jnp.float32)
        / SOFTMAX_TEMPER
        - log_sample_share[None, :]
    )
    allowed_items = pos_ids[0][:, None] != all_ids[None, :]
    terms = jnp.where(allowed_items, jnp.exp(score_logits), 0.0)
    pos_exp = jnp.exp(positive_item)
    denom = pos_exp + jnp.sum(terms, axis=1)
    loss = jnp.log(denom) - positive_item
    positive_gradient = pos_exp / denom - 1.0
    probabilities = (terms / denom[:, None]).astype(jnp.bfloat16)
    user_gradient = (
        positive_gradient[:, None] * positive_unit / SOFTMAX_TEMPER
        + jnp.dot(probabilities, every_unit_vector, preferred_element_type=jnp.float32)
        / SOFTMAX_TEMPER
    )
    unit_gradient = (
        jnp.einsum("wz,wb->zb", probabilities, user_rounded, preferred_element_type=jnp.float32)
        / SOFTMAX_TEMPER
    )
    owned = lax.psum_scatter(
        unit_gradient.astype(jnp.bfloat16), "batch", scatter_dimension=0, tiled=True
    ).astype(jnp.float32)
    d_total = lax.psum(owned, "ctx")
    d_neg = neg_scale * (d_total - neg_unit * jnp.sum(neg_unit * d_total, axis=1, keepdims=True))
    d_outputs = out_scale * (
        user_gradient - user_vector * jnp.sum(user_vector * user_gradient, axis=1, keepdims=True)
    )
    d_gated = jnp.einsum(
        "ik,dk->id", d_outputs.astype(jnp.bfloat16), w_out, preferred_element_type=jnp.float32
    )
    d_normed = d_gated * gate_u
    d_gate = d_gated * normed
    d_mixed = inv_std * (
        d_normed
        - jnp.mean(d_normed, axis=1, keepdims=True)
        - normed * jnp.mean(d_normed * normed, axis=1, keepdims=True)
    )
    d_rows = d_mixed.astype(jnp.bfloat16)
    d_heads = split_heads(d_rows)

    def query_step(index, carry):
        start = index * block_rows
        keys_blk = lax.dynamic_slice_in_dim(heads_keys, start, block_rows, 0)
        values_blk = lax.dynamic_slice_in_dim(heads_values, start, block_rows, 0)
        scores = (
            jnp.einsum("ihe,jhe->hij", local_q, keys_blk, preferred_element_type=jnp.float32)
            * score_scale
        )
        allowed = ((start + lax.iota(jnp.int32, block_rows))[None, :] <= row_pos[:, None])[None]
        d_weights = jnp.einsum(
            "ihe,jhe->hij", d_heads, values_blk, preferred_element_type=jnp.float32
        )
        d_scores = jnp.where(allowed, d_weights * silu_slope(scores) * score_scale, 0.0).astype(
            jnp.bfloat16
        )
        return carry + jnp.einsum(
            "hij,jhe->ihe", d_scores, keys_blk, preferred_element_type=jnp.float32
        )

    d_queries = lax.fori_loop(0, length // block_rows, query_step, empty)
    queries_piece = lax.all_gather(query_rows, "ctx", axis=0, tiled=True)
    grads_piece = lax.all_gather(d_rows, "ctx", axis=0, tiled=True)
    count = queries_piece.shape[0]
    inner = math.gcd(count, 512)

    def inner_step(index, sums):
        first = index * inner
        query_blk = split_heads(lax.dynamic_slice_in_dim(queries_piece, first, inner, 0))
        grad_blk = split_heads(lax.dynamic_slice_in_dim(grads_piece, first, inner, 0))
        query_pos = first + lax.iota(jnp.int32, inner)
        scores = (
            jnp.einsum("ihe,jhe->hij", query_blk, local_k, preferred_element_type=jnp.float32)
            * score_scale
        )
        allowed = (row_pos[None, :] <= query_pos[:, None])[None]
        weights = jnp.where(allowed, jax.nn.silu(scores), 0.0).astype(jnp.bfloat16)
        d_weights = jnp.einsum(
            "ihe,jhe->hij", grad_blk, local_v, preferred_element_type=jnp.float32
        )
        d_scores = jnp.where(allowed, d_weights * silu_slope(scores) * score_scale, 0.0).astype(
            jnp.bfloat16
        )
        new_keys = sums[0] + jnp.einsum(
            "hij,ihe->jhe", d_scores, query_blk, preferred_element_type=jnp.float32
        )
        new_values = sums[1] + jnp.einsum(
            "hij,ihe->jhe", weights, grad_blk, preferred_element_type=jnp.float32
        )
        return (new_keys, new_values)

    d_keys, d_values = lax.fori_loop(0, count // inner, inner_step, (empty, empty))
    d_proj = jnp.concatenate(
        [
            d_gate,
            d_values.reshape(tokens, D),
            d_queries.reshape(tokens, D),
            d_keys.reshape(tokens, D),
        ],
        axis=1,
    )
    d_pre = (d_proj * silu_slope(pre_act)).astype(jnp.bfloat16)
    d_seq = (
        d_outputs + jnp.einsum("ik,dk->id", d_pre, w_in, preferred_element_type=jnp.float32)
    ).astype(jnp.bfloat16)
    return (loss[None], d_seq[None], d_neg)


def solution(mesh):
    in_specs = (
        P("batch", "ctx", None),
        P(),
        P(),
        P("batch", "ctx", None),
        P("batch", "ctx"),
        P("batch", None),
        P("batch"),
        P("batch"),
    )
    out_specs = (P("batch", "ctx"), P("batch", "ctx", None), P("batch", None))
    return jax.shard_map(shards, mesh=mesh, in_specs=in_specs, out_specs=out_specs, check_vma=False)
```

profile of v0, /device:TPU:1, one launch (start us, length us, event | category | flops | bytes accessed | tf_op | source)
XLA Modules:
  0.0 607.7 jit_solution(220923983265694282)
XLA Ops:
  8.8 2.4 multiply_convert_fusion
  15.3 19.5 %all-reduce.2 = (s32[128]{0:T(128)S(1)}, s32[128]{0:T(128)}) all-reduce(s32[128]{0:T(128)S(1)} %dynamic-update-slice.1, s32[128]{0:T(128)S(1)} %dynamic-update-slice), channel_id=1, replica_groups=mesh['ctx'=32,'batch'=16] {'batch'}, use_global_device_ids=true, to_apply=%add.1 | all-reduce | flops 256 | bytes 2048
  35.0 26.8 %all_gather.24 = bf16[128,512]{1,0:T(8,128)(2,1)} all-gather(bf16[8,512]{1,0:T(8,128)(2,1)S(1)} %fusion.98), channel_id=1, replica_groups=mesh['ctx'=32,'batch'=16] {'batch'}, dimensions={0}, use_global_device_ids=true | all-gather | bytes 139264 | tf_op jit(solution)/shard_map/all_gather | solution.py:31
  64.2 45.5 %all-gather.5.cloned.1.call-done = bf16[4096,512]{1,0:T(8,128)(2,1)} async-done(((bf16[128,512]{1,0:T(8,128)(2,1)}), bf16[4096,512]{1,0:T(8,128)(2,1)}) %all-gather.5.cloned.1.call-update) | async-done | bytes 4194320 | tf_op jit(solution)/shard_map/all_gather | solution.py:45
  109.7 6.4 %copy.27 = bf16[4096,512]{0,1:T(8,128)(2,1)} copy(bf16[4096,512]{1,0:T(8,128)(2,1)} %all-gather.5.cloned.1.call-done) | data formatting | bytes 8388608 | tf_op jit(solution)/shard_map/all_gather | solution.py:45
  116.1 86.6 %all-gather.7.cloned.1.call-done = bf16[4096,512]{1,0:T(8,128)(2,1)} async-done(((bf16[128,512]{1,0:T(8,128)(2,1)}), bf16[4096,512]{1,0:T(8,128)(2,1)}) %all-gather.7.cloned.1.call-update) | async-done | bytes 4194320 | tf_op jit(solution)/shard_map/all_gather | solution.py:46
  202.7 6.4 %copy.28 = bf16[4096,512]{0,1:T(8,128)(2,1)} copy(bf16[4096,512]{1,0:T(8,128)(2,1)} %all-gather.7.cloned.1.call-done) | data formatting | bytes 8388608 | tf_op jit(solution)/shard_map/all_gather | solution.py:46
  209.1 19.7 %while.44 = (s32[]{:T(128)}, f32[128,8,64]{0,2,1:T(8,128)S(1)}, bf16[4096,8,64]{0,2,1:T(8,128)(2,1)}, bf16[4096,8,64]{0,2,1:T(8,128)(2,1)}, bf16[128,8,64]{0,2,1...) while((s32[]{:T(128)}, f32[128,8,64]{0,2,1:T(8,128)S(1)}, ...), condition=%wide.region_1.0_spmd.clone, body=%wide.region_0.0_spmd.clone.sunk | while | flops 138084992 | bytes 1841828 | solution.py:71
  209.2 2.3 fusion.146
  211.7 2.3 fusion.146
  214.2 2.3 fusion.146
  216.6 2.3 fusion.146
  219.1 2.3 fusion.146
  221.6 2.3 fusion.146
  224.1 2.3 fusion.146
  226.5 2.3 fusion.146
  238.3 1.8 copy.35
  242.7 1.7 fusion.86
  245.2 57.4 %while.46 = (s32[]{:T(128)}, f32[128,8,64]{0,2,1:T(8,128)}, bf16[4096,8,64]{0,2,1:T(8,128)(2,1)}, bf16[4096,8,64]{0,2,1:T(8,128)(2,1)}, bf16[128,8,64]{2,1,0:T(8...) while((s32[]{:T(128)}, f32[128,8,64]{0,2,1:T(8,128)}, ...), condition=%wide.region_16.17_spmd.clone, body=%wide.region_15.16_spmd.clone.sunk | while | flops 207815296 | bytes 9313028 | solution.py:146
  245.2 2.9 fusion.161
  248.3 3.3 fusion.162
  252.4 2.9 fusion.161
  255.5 3.3 fusion.162
  259.5 2.9 fusion.161
  262.6 3.4 fusion.162
  266.7 2.9 fusion.161
  269.8 3.4 fusion.162
  273.9 2.9 fusion.161
  277.0 3.4 fusion.162
  281.1 2.9 fusion.161
  284.2 3.3 fusion.162
  288.2 2.9 fusion.161
  291.3 3.3 fusion.162
  295.4 2.9 fusion.161
  298.5 3.3 fusion.162
  302.6 1.8 copy.40
  304.9 125.1 %psum.7 = f32[8,512]{1,0:T(8,128)S(1)} all-reduce(bf16[8,512]{1,0:T(8,128)(2,1)} %reduce-scatter.2.cloned.1.call-done), channel_id=1, replica_groups=mesh['ctx'=32,'batch'=16] {'ctx'}, use_global_device_ids=true, to_apply=%region_18.19 | all-reduce | flops 4096 | bytes 24576 | tf_op jit(solution)/shard_map/psum | solution.py:109
  430.8 61.0 %all-gather.11.cloned.1.call-done = bf16[4096,512]{1,0:T(8,128)(2,1)} async-done(((bf16[128,512]{1,0:T(8,128)(2,1)}), bf16[4096,512]{1,0:T(8,128)(2,1)}) %all-gather.11.cloned.1.call-update) | async-done | bytes 4194320 | tf_op jit(solution)/shard_map/all_gather | solution.py:148
  491.8 104.2 %while.45 = (s32[]{:T(128)}, f32[128,8,64]{0,2,1:T(8,128)}, f32[128,8,64]{0,2,1:T(8,128)}, bf16[4096,512]{1,0:T(8,128)(2,1)}, bf16[4096,512]{1,0:T(8,128)(2,1)},...) while((s32[]{:T(128)}, f32[128,8,64]{0,2,1:T(8,128)}, ...), condition=%wide.region_14.15_spmd.clone, body=%wide.region_13.14_spmd.clone.sunk | while | flops 278725248 | bytes 16192726 | solution.py:177
  494.1 2.9 fusion.153
  498.0 3.1 fusion.155
  501.2 3.6 fusion.154
  507.1 2.9 fusion.153
  511.0 3.1 fusion.155
  514.1 3.7 fusion.154
  520.1 2.9 fusion.153
  524.0 3.1 fusion.155
  527.1 3.7 fusion.154
  533.1 2.9 fusion.153
  537.0 3.1 fusion.155
  540.2 3.7 fusion.154
  546.2 2.9 fusion.153
  550.1 3.1 fusion.155
  553.2 3.7 fusion.154
  559.2 2.9 fusion.153
  563.1 3.1 fusion.155
  566.3 3.7 fusion.154
  572.2 2.9 fusion.153
  576.1 3.1 fusion.155
  579.3 3.7 fusion.154
  585.3 2.9 fusion.153
  589.2 3.1 fusion.155
  592.3 3.7 fusion.154
  598.2 2.9 fusion.74
  (263 shorter events, 57.8 us)
Async XLA Ops:
  7.2 1.6 copy-start
  7.2 7.6 %copy-start.27 = (s32[8]{0:T(128)S(1)}, s32[8]{0:T(128)}, u32[]{:S(2)}) copy-start(s32[8]{0:T(128)} %param.20) | copy-start | bytes 100
  7.2 7.9 %copy-start.28 = (s32[8]{0:T(128)S(1)}, s32[8]{0:T(128)}, u32[]{:S(2)}) copy-start(s32[8]{0:T(128)} %param.21) | copy-start | bytes 100
  7.2 27.6 %copy-start.15 = (bf16[8,512]{1,0:T(8,128)(2,1)S(1)}, bf16[8,512]{1,0:T(8,128)(2,1)}, u32[]{:S(2)}) copy-start(bf16[8,512]{1,0:T(8,128)(2,1)} %param.19) | copy-start | bytes 24580
  7.2 55.1 %copy-start.3 = (bf16[1,128,512]{2,1,0:T(8,128)(2,1)S(1)}, bf16[1,128,512]{2,1,0:T(8,128)(2,1)}, u32[]{:S(2)}) copy-start(bf16[1,128,512]{2,1,0:T(8,128)(2,1)} %param.17) | copy-start | bytes 393220
  7.2 102.5 %all-gather.5.cloned.1.call-start = ((), (), s32[]{:S(2)}) async-start(), calls=%async_computation.1 | async-start | bytes 4325376 | tf_op jit(solution)/shard_map/all_gather | solution.py:45
  11.1 1.6 copy-start.6
  11.9 104.2 %copy-start.5 = (bf16[128,512]{1,0:T(8,128)(2,1)}, bf16[128,512]{1,0:T(8,128)(2,1)S(1)}, u32[]{:S(2)}) copy-start(bf16[128,512]{1,0:T(8,128)(2,1)S(1)} %get-tuple-element.547) | copy-start | bytes 393220
  11.9 190.8 %all-gather.7.cloned.1.call-start = ((), (), s32[]{:S(2)}) async-start(), calls=%async_computation.2 | async-start | bytes 4325376 | tf_op jit(solution)/shard_map/all_gather | solution.py:46
  12.7 292.2 %reduce-scatter.2.cloned.1.call-start = ((), (), s32[]{:S(2)}) async-start(), calls=%async_computation.5 | async-start | bytes 139264 | tf_op jit(solution)/shard_map/reduce_scatter | solution.py:106
  34.9 81.2 %copy-start.19 = (f32[8]{0:T(128)}, f32[8]{0:T(128)S(1)}, u32[]{:S(2)}) copy-start(f32[8]{0:T(128)S(1)} %add_rsqrt_fusion) | copy-start | bytes 100
  209.1 20.5 %copy-start.2 = (bf16[512,512]{1,0:T(8,128)(2,1)S(1)}, bf16[512,512]{1,0:T(8,128)(2,1)}, u32[]{:S(2)}) copy-start(bf16[512,512]{1,0:T(8,128)(2,1)} %param.16) | copy-start | bytes 1572868
  228.8 0.7 copy-start.13
  229.5 1.5 copy-start.16
  229.6 10.5 %copy-start.4 = (bf16[1,128,512]{2,1,0:T(8,128)(2,1)S(1)}, bf16[1,128,512]{2,1,0:T(8,128)(2,1)}, u32[]{:S(2)}) copy-start(bf16[1,128,512]{2,1,0:T(8,128)(2,1)} %param.17) | copy-start | bytes 393220
  229.6 10.5 %copy-start.7 = (bf16[128,512]{1,0:T(8,128)(2,1)S(1)}, bf16[128,512]{1,0:T(8,128)(2,1)}, u32[]{:S(2)}) copy-start(bf16[128,512]{1,0:T(8,128)(2,1)} %all_gather.24) | copy-start | bytes 393220
  231.7 0.5 copy-start.17
  231.9 1.5 copy-start.23
  233.4 0.6 copy-start.10
  233.4 2.2 copy-start.25
  234.0 1.6 copy-start.18
  235.0 195.9 %all-gather.9.cloned.1.call-start = ((), (), s32[]{:S(2)}) async-start(), calls=%async_computation.3 | async-start | bytes 4325376 | tf_op jit(solution)/shard_map/all_gather | solution.py:147
  235.5 256.3 %all-gather.11.cloned.1.call-start = ((), (), s32[]{:S(2)}) async-start(), calls=%async_computation.4 | async-start | bytes 4325376 | tf_op jit(solution)/shard_map/all_gather | solution.py:148
  241.2 3.2 copy-start.9
  241.3 3.2 copy-start.21
  244.5 0.7 copy-start.8
  245.1 59.2 %copy-start.24 = (f32[128]{0:T(128)S(1)}, f32[128]{0:T(128)}, u32[]{:S(2)}) copy-start(f32[128]{0:T(128)} %copy-done.23) | copy-start | bytes 1540
  245.2 59.2 %copy-start.26 = (f32[128]{0:T(128)S(1)}, f32[128]{0:T(128)}, u32[]{:S(2)}) copy-start(f32[128]{0:T(128)} %copy-done.25) | copy-start | bytes 1540
  245.2 184.8 %copy-start.20 = (f32[8]{0:T(128)S(1)}, f32[8]{0:T(128)}, u32[]{:S(2)}) copy-start(f32[8]{0:T(128)} %copy-done.19) | copy-start | bytes 100
  245.2 3.1 copy-start.11
  245.2 3.1 copy-start.14
  251.7 0.7 copy-start.12
  252.4 3.1 copy-start.11
  252.4 3.1 copy-start.14
  258.8 0.7 copy-start.12
  259.5 3.1 copy-start.11
  259.5 3.1 copy-start.14
  266.0 0.7 copy-start.12
  266.7 3.1 copy-start.11
  266.7 3.1 copy-start.14
  273.2 0.7 copy-start.12
  273.9 3.1 copy-start.11
  273.9 3.1 copy-start.14
  280.4 0.7 copy-start.12
  281.1 3.1 copy-start.11
  281.1 3.1 copy-start.14
  287.5 0.7 copy-start.12
  288.2 3.1 copy-start.11
  288.2 3.1 copy-start.14
  294.7 0.7 copy-start.12
  295.4 3.1 copy-start.11
  295.4 3.1 copy-start.14
  301.9 0.7 copy-start.12
  491.8 106.4 %copy-start.22 = (f32[128]{0:T(128)S(1)}, f32[128]{0:T(128)}, u32[]{:S(2)}) copy-start(f32[128]{0:T(128)} %copy-done.21) | copy-start | bytes 1540
  498.0 3.1 copy-start.1
  511.0 3.2 copy-start.1
  524.0 3.2 copy-start.1
  537.0 3.2 copy-start.1
  550.1 3.2 copy-start.1
  563.1 3.2 copy-start.1
  576.1 3.2 copy-start.1
  589.2 3.2 copy-start.1
Sparse Core Ops, SparseCore 0:
  12.0 97.6 all-gather.4
  113.7 88.9 all-gather.6
  235.1 58.7 reduce-scatter.1
  297.1 101.8 all-gather.8
  402.8 88.9 all-gather.10
where the time goes:
time: 610 us; the launch traced here: 608 us
  waiting for transfers between devices  194 us (32%)
  blocking collectives  171 us (28%)
  matrix products  158 us (26%)
  local copies, waits for them, and re-layouts  52.5 us (9%)
  other arithmetic  15.9 us (3%)
  between operations  14.8 us (2%)
    psum x1, blocking collectives, shards(): d_total = lax.psum(owned, 'ctx')  125 us
    all_gather x1, waiting for transfers between devices, shards(): lax.all_gather(key_rows, 'ctx', axis=0, tiled=True)  86.6 us
    all_gather x1, waiting for transfers between devices, shards(): grads_piece = lax.all_gather(d_rows, 'ctx', axis=0, tiled=True)  61 us
    all_gather x1, waiting for transfers between devices, shards(): lax.all_gather(value_rows, 'ctx', axis=0, tiled=True)  45.5 us
    dot_general x8, matrix products, inner_step(): jnp.einsum('hij,ihe->jhe', d_scores, query_blk, preferred_element_type=jn...  29.6 us
    dot_general x8, matrix products, query_step(): jnp.einsum('hij,jhe->ihe', d_scores, keys_blk, preferred_element_type=jnp...  26.8 us
    all_gather x1, blocking collectives, shards(): lax.all_gather(neg_unit.astype(jnp.bfloat16), 'batch', axis=0, tiled=True)  26.8 us
    dot_general x8, matrix products, inner_step(): jnp.einsum('hij,ihe->jhe', weights, grad_blk, preferred_element_type=jnp....  25.2 us
  transfers between devices with their start and end apart: 5, of which 3 were waited for; matrix products, arithmetic and copies ran while one was open for 12% of the time, Pallas kernels for 0%

commit v1 on v0

--- a/solution.py
+++ b/solution.py
@@ -42,7 +42,9 @@
     query_rows = proj[:, 2 * D : 3 * D]
     key_rows = proj[:, 3 * D :]
     all_values, all_keys = (
-        lax.all_gather(value_rows, "ctx", axis=0, tiled=True),
+        jnp.concatenate(
+            lax.all_to_all(jnp.stack([value_rows] * lax.axis_size("ctx")), "ctx", 0, 0), axis=0
+        ),
         lax.all_gather(key_rows, "ctx", axis=0, tiled=True),
     )
     length = all_keys.shape[0]

time: 610 us -> 560 us (0.918)
  waiting for transfers between devices: 194 us -> 115 us
  starting transfers between devices: 0.2 us -> 11.6 us
  blocking collectives: 171 us -> 181 us
  local copies, waits for them, and re-layouts: 52.5 us -> 60.7 us
    all_gather x1, waiting for transfers between devices: 86.6 us -> 2.96 us  [shards(): lax.all_gather(key_rows, 'ctx', axis=0, tiled=True)]
    all_to_all x0 -> x1, waiting for transfers between devices: none -> 49 us  [shards(): lax.all_to_all(jnp.stack([value_rows] * lax.axis_size('ctx')), 'ctx', 0, 0)]
    all_gather x1 -> x0, waiting for transfers between devices: 45.5 us -> none  [shards(): lax.all_gather(value_rows, 'ctx', axis=0, tiled=True)]
    all_to_all x0 -> x1, starting transfers between devices: none -> 11.4 us  [shards(): lax.all_to_all(jnp.stack([value_rows] * lax.axis_size('ctx')), 'ctx', 0, 0)]
    another operation x0 -> x2, local copies, waits for them, and re-layouts: none -> 10.2 us  [the longest x1 7.33 us: split_heads(): return matrix.reshape(matrix.shape[0], HEADS, HEAD)]
    all_to_all x0 -> x1, local copies, waits for them, and re-layouts: none -> 6.81 us  [shards(): lax.all_to_all(jnp.stack([value_rows] * lax.axis_size('ctx')), 'ctx', 0, 0)]
    all_gather x1 -> x0, local copies, waits for them, and re-layouts: 6.36 us -> none  [shards(): lax.all_gather(value_rows, 'ctx', axis=0, tiled=True)]
  transfers between devices with their start and end apart: 5 -> 5, of which waited for: 3 -> 3; matrix products, arithmetic and copies ran while one was open for 12% -> 14% of each run, Pallas kernels for 0% -> 0%
where the time goes in v1:
time: 560 us; the launch traced here: 558 us
  blocking collectives  181 us (32%)
  matrix products  158 us (28%)
  waiting for transfers between devices  115 us (21%)
  local copies, waits for them, and re-layouts  60.7 us (11%)
  other arithmetic  15.9 us (3%)
  between operations  14.8 us (3%)
  starting transfers between devices  11.6 us (2%)
    psum x1, blocking collectives, shards(): d_total = lax.psum(owned, 'ctx')  131 us
    all_gather x1, waiting for transfers between devices, shards(): grads_piece = lax.all_gather(d_rows, 'ctx', axis=0, tiled=True)  61.4 us
    all_to_all x1, waiting for transfers between devices, shards(): lax.all_to_all(jnp.stack([value_rows] * lax.axis_size('ctx')), 'ctx', 0, 0)  49 us
    dot_general x8, matrix products, inner_step(): jnp.einsum('hij,ihe->jhe', d_scores, query_blk, preferred_element_type=jn...  29.4 us
    all_gather x1, blocking collectives, shards(): lax.all_gather(neg_unit.astype(jnp.bfloat16), 'batch', axis=0, tiled=True)  28.7 us
    dot_general x8, matrix products, query_step(): jnp.einsum('hij,jhe->ihe', d_scores, keys_blk, preferred_element_type=jnp...  26.8 us
    dot_general x8, matrix products, inner_step(): jnp.einsum('hij,ihe->jhe', weights, grad_blk, preferred_element_type=jnp....  25.1 us
    dot_general x8, matrix products, query_step(): jnp.einsum('ihe,jhe->hij', d_heads, values_blk, preferred_element_type=jn...  23.5 us
  transfers between devices with their start and end apart: 5, of which 3 were waited for; matrix products, arithmetic and copies ran while one was open for 14% of the time, Pallas kernels for 0%

profile of v1, /device:TPU:1, one launch (start us, length us, event | category | flops | bytes accessed | tf_op | source)
XLA Modules:
  0.0 557.8 jit_solution(12414135449150090509)
XLA Ops:
  8.8 2.4 multiply_convert_fusion
  12.7 2.9 stack.2
  15.7 11.4 %all-to-all-start = ((bf16[32,128,512]{1,2,0:T(8,128)(2,1)}), bf16[32,128,512]{1,2,0:T(8,128)(2,1)}, u32[]{:S(2)}, u32[]{:S(2)}) async-start(bf16[32,128,512]{1,2,0:T(8,128)(2,1)} %stack.2), calls=%async_computation | async-start | bytes 8388608 | tf_op jit(solution)/shard_map/all_to_all | solution.py:46
  30.5 21.6 %all-reduce.2 = (s32[128]{0:T(128)S(1)}, s32[128]{0:T(128)}) all-reduce(s32[128]{0:T(128)S(1)} %dynamic-update-slice.1, s32[128]{0:T(128)S(1)} %dynamic-update-slice), channel_id=1, replica_groups=mesh['ctx'=32,'batch'=16] {'batch'}, use_global_device_ids=true, to_apply=%add.1 | all-reduce | flops 256 | bytes 2048
  52.3 28.7 %all_gather.20 = bf16[128,512]{1,0:T(8,128)(2,1)} all-gather(bf16[8,512]{1,0:T(8,128)(2,1)S(1)} %fusion.95), channel_id=1, replica_groups=mesh['ctx'=32,'batch'=16] {'batch'}, dimensions={0}, use_global_device_ids=true | all-gather | bytes 139264 | tf_op jit(solution)/shard_map/all_gather | solution.py:31
  83.4 49.0 %all-to-all-done = bf16[32,128,512]{1,2,0:T(8,128)(2,1)} async-done(((bf16[32,128,512]{1,2,0:T(8,128)(2,1)}), bf16[32,128,512]{1,2,0:T(8,128)(2,1)}, u32[]{:S(2)}, u32[]{:S(2)}) %all-to-all-start) | async-done | bytes 4194336 | tf_op jit(solution)/shard_map/all_to_all | solution.py:46
  132.4 6.8 %copy.45 = bf16[32,128,512]{1,0,2:T(8,128)(2,1)} copy(bf16[32,128,512]{1,2,0:T(8,128)(2,1)} %all-to-all-done) | data formatting | bytes 8388608 | tf_op jit(solution)/shard_map/all_to_all | solution.py:46
  139.2 7.3 %reshape_reshape.3 = bf16[4096,8,64]{0,2,1:T(8,128)(2,1)} reshape(bf16[32,128,512]{1,0,2:T(8,128)(2,1)} %copy.45) | data formatting | bytes 8388608 | tf_op jit(solution)/shard_map/reshape;reshape | solution.py:19
  146.5 3.0 all-gather.4.cloned.1.call-done
  149.5 6.4 %copy.46 = bf16[4096,512]{0,1:T(8,128)(2,1)} copy(bf16[4096,512]{1,0:T(8,128)(2,1)} %all-gather.4.cloned.1.call-done) | data formatting | bytes 8388608 | tf_op jit(solution)/shard_map/all_gather | solution.py:48
  155.8 19.7 %while.44 = (s32[]{:T(128)}, f32[128,8,64]{0,2,1:T(8,128)S(1)}, bf16[4096,8,64]{0,2,1:T(8,128)(2,1)}, bf16[4096,8,64]{0,2,1:T(8,128)(2,1)}, bf16[128,8,64]{0,2,1...) while((s32[]{:T(128)}, f32[128,8,64]{0,2,1:T(8,128)S(1)}, ...), condition=%wide.region_1.0_spmd.clone, body=%wide.region_0.0_spmd.clone.sunk | while | flops 138084992 | bytes 1841828 | solution.py:73
  156.0 2.3 fusion.145
  158.5 2.3 fusion.145
  160.9 2.3 fusion.145
  163.4 2.3 fusion.145
  165.9 2.3 fusion.145
  168.4 2.3 fusion.145
  170.8 2.3 fusion.145
  173.3 2.3 fusion.145
  188.9 57.4 %while.46 = (s32[]{:T(128)}, f32[128,8,64]{0,2,1:T(8,128)}, bf16[4096,8,64]{0,2,1:T(8,128)(2,1)}, bf16[4096,8,64]{0,2,1:T(8,128)(2,1)}, bf16[128,8,64]{0,2,1:T(8...) while((s32[]{:T(128)}, f32[128,8,64]{0,2,1:T(8,128)}, ...), condition=%wide.region_16.17_spmd.clone, body=%wide.region_15.16_spmd.clone.sunk | while | flops 207815296 | bytes 9313028 | solution.py:148
  188.9 2.9 fusion.160
  192.0 3.3 fusion.161
  196.1 2.9 fusion.160
  199.2 3.3 fusion.161
  203.3 2.9 fusion.160
  206.4 3.4 fusion.161
  210.5 2.9 fusion.160
  213.6 3.4 fusion.161
  217.6 2.9 fusion.160
  220.7 3.4 fusion.161
  224.8 2.9 fusion.160
  227.9 3.3 fusion.161
  232.0 2.9 fusion.160
  235.1 3.3 fusion.161
  239.2 2.9 fusion.160
  242.3 3.4 fusion.161
  248.7 131.0 %psum.7 = f32[8,512]{1,0:T(8,128)S(1)} all-reduce(bf16[8,512]{1,0:T(8,128)(2,1)} %reduce-scatter.2.cloned.1.call-done), channel_id=1, replica_groups=mesh['ctx'=32,'batch'=16] {'ctx'}, use_global_device_ids=true, to_apply=%region_18.19 | all-reduce | flops 4096 | bytes 24576 | tf_op jit(solution)/shard_map/psum | solution.py:111
  380.5 61.4 %all-gather.8.cloned.1.call-done = bf16[4096,512]{1,0:T(8,128)(2,1)} async-done(((bf16[128,512]{1,0:T(8,128)(2,1)}), bf16[4096,512]{1,0:T(8,128)(2,1)}) %all-gather.8.cloned.1.call-update) | async-done | bytes 4194320 | tf_op jit(solution)/shard_map/all_gather | solution.py:150
  441.9 104.2 %while.45 = (s32[]{:T(128)}, f32[128,8,64]{0,2,1:T(8,128)}, f32[128,8,64]{0,2,1:T(8,128)}, bf16[4096,512]{1,0:T(8,128)(2,1)}, bf16[4096,512]{1,0:T(8,128)(2,1)},...) while((s32[]{:T(128)}, f32[128,8,64]{0,2,1:T(8,128)}, ...), condition=%wide.region_14.15_spmd.clone, body=%wide.region_13.14_spmd.clone.sunk | while | flops 278725248 | bytes 16192726 | solution.py:179
  444.2 2.9 fusion.152
  448.1 3.1 fusion.154
  451.2 3.6 fusion.153
  457.1 2.9 fusion.152
  461.1 3.1 fusion.154
  464.2 3.7 fusion.153
  470.2 2.9 fusion.152
  474.1 3.1 fusion.154
  477.3 3.7 fusion.153
  483.2 2.9 fusion.152
  487.1 3.1 fusion.154
  490.3 3.7 fusion.153
  496.3 2.9 fusion.152
  500.2 3.1 fusion.154
  503.3 3.7 fusion.153
  509.3 2.9 fusion.152
  513.2 3.1 fusion.154
  516.4 3.7 fusion.153
  522.3 2.9 fusion.152
  526.3 3.1 fusion.154
  529.4 3.7 fusion.153
  535.4 2.9 fusion.152
  539.3 3.1 fusion.154
  542.4 3.7 fusion.153
  548.3 2.9 fusion.71
  (260 shorter events, 61.0 us)
Async XLA Ops:
  7.2 1.6 copy-start
  11.1 0.8 copy-start.5
  12.6 15.3 %copy-start.4 = (bf16[128,512]{1,0:T(8,128)(2,1)}, bf16[128,512]{1,0:T(8,128)(2,1)S(1)}, u32[]{:S(2)}) copy-start(bf16[128,512]{1,0:T(8,128)(2,1)S(1)} %get-tuple-element.555) | copy-start | bytes 393220
  12.7 2.9 copy-start.9
  15.7 14.3 %copy-start.26 = (s32[8]{0:T(128)S(1)}, s32[8]{0:T(128)}, u32[]{:S(2)}) copy-start(s32[8]{0:T(128)} %param.20) | copy-start | bytes 100
  15.7 14.6 %copy-start.27 = (s32[8]{0:T(128)S(1)}, s32[8]{0:T(128)}, u32[]{:S(2)}) copy-start(s32[8]{0:T(128)} %param.21) | copy-start | bytes 100
  15.7 36.4 %copy-start.14 = (bf16[8,512]{1,0:T(8,128)(2,1)S(1)}, bf16[8,512]{1,0:T(8,128)(2,1)}, u32[]{:S(2)}) copy-start(bf16[8,512]{1,0:T(8,128)(2,1)} %param.19) | copy-start | bytes 24580
  15.7 65.9 %copy-start.3 = (bf16[1,128,512]{2,1,0:T(8,128)(2,1)S(1)}, bf16[1,128,512]{2,1,0:T(8,128)(2,1)}, u32[]{:S(2)}) copy-start(bf16[1,128,512]{2,1,0:T(8,128)(2,1)} %param.17) | copy-start | bytes 393220
  15.7 116.7 %all-to-all-start = ((bf16[32,128,512]{1,2,0:T(8,128)(2,1)}), bf16[32,128,512]{1,2,0:T(8,128)(2,1)}, u32[]{:S(2)}, u32[]{:S(2)}) async-start(bf16[32,128,512]{1,2,0:T(8,128)(2,1)} %stack.2), calls=%async_computation | async-start | bytes 8388608 | tf_op jit(solution)/shard_map/all_to_all | solution.py:46
  27.1 122.4 %all-gather.4.cloned.1.call-start = ((), (), s32[]{:S(2)}) async-start(), calls=%async_computation.2 | async-start | bytes 4325376 | tf_op jit(solution)/shard_map/all_gather | solution.py:48
  27.8 220.8 %reduce-scatter.2.cloned.1.call-start = ((), (), s32[]{:S(2)}) async-start(), calls=%async_computation.5 | async-start | bytes 139264 | tf_op jit(solution)/shard_map/reduce_scatter | solution.py:108
  52.2 87.0 %copy-start.18 = (f32[8]{0:T(128)}, f32[8]{0:T(128)S(1)}, u32[]{:S(2)}) copy-start(f32[8]{0:T(128)S(1)} %add_rsqrt_fusion) | copy-start | bytes 100
  155.8 20.5 %copy-start.2 = (bf16[512,512]{1,0:T(8,128)(2,1)S(1)}, bf16[512,512]{1,0:T(8,128)(2,1)}, u32[]{:S(2)}) copy-start(bf16[512,512]{1,0:T(8,128)(2,1)} %param.16) | copy-start | bytes 1572868
  175.6 0.7 copy-start.12
  176.2 1.5 copy-start.15
  178.4 0.6 copy-start.16
  178.6 5.0 copy-start.22
  180.2 2.3 copy-start.24
  180.2 3.4 copy-start.8
  180.8 1.7 copy-start.17
  181.7 198.8 %all-gather.6.cloned.1.call-start = ((), (), s32[]{:S(2)}) async-start(), calls=%async_computation.3 | async-start | bytes 4325376 | tf_op jit(solution)/shard_map/all_gather | solution.py:149
  182.5 259.4 %all-gather.8.cloned.1.call-start = ((), (), s32[]{:S(2)}) async-start(), calls=%async_computation.4 | async-start | bytes 4325376 | tf_op jit(solution)/shard_map/all_gather | solution.py:150
  184.9 1.5 copy-start.7
  185.0 3.2 copy-start.20
  188.2 0.7 copy-start.6
  188.9 59.3 %copy-start.23 = (f32[128]{0:T(128)S(1)}, f32[128]{0:T(128)}, u32[]{:S(2)}) copy-start(f32[128]{0:T(128)} %copy-done.22) | copy-start | bytes 1540
  188.9 59.3 %copy-start.25 = (f32[128]{0:T(128)S(1)}, f32[128]{0:T(128)}, u32[]{:S(2)}) copy-start(f32[128]{0:T(128)} %copy-done.24) | copy-start | bytes 1540
  188.9 190.7 %copy-start.19 = (f32[8]{0:T(128)S(1)}, f32[8]{0:T(128)}, u32[]{:S(2)}) copy-start(f32[8]{0:T(128)} %copy-done.18) | copy-start | bytes 100
  188.9 3.1 copy-start.10
  188.9 3.1 copy-start.13
  195.4 0.7 copy-start.11
  196.1 3.1 copy-start.10
  196.1 3.1 copy-start.13
  202.6 0.7 copy-start.11
  203.3 3.1 copy-start.10
  203.3 3.1 copy-start.13
  209.7 0.7 copy-start.11
  210.4 3.1 copy-start.10
  210.5 3.1 copy-start.13
  216.9 0.7 copy-start.11
  217.6 3.1 copy-start.10
  217.6 3.1 copy-start.13
  224.1 0.7 copy-start.11
  224.8 3.1 copy-start.10
  224.8 3.1 copy-start.13
  231.3 0.7 copy-start.11
  232.0 3.1 copy-start.10
  232.0 3.1 copy-start.13
  238.4 0.7 copy-start.11
  239.1 3.1 copy-start.10
  239.2 3.1 copy-start.13
  245.6 0.7 copy-start.11
  441.9 106.4 %copy-start.21 = (f32[128]{0:T(128)S(1)}, f32[128]{0:T(128)}, u32[]{:S(2)}) copy-start(f32[128]{0:T(128)} %copy-done.20) | copy-start | bytes 1540
  448.1 3.1 copy-start.1
  461.1 3.1 copy-start.1
  474.1 3.1 copy-start.1
  487.1 3.1 copy-start.1
  500.2 3.1 copy-start.1
  513.2 3.1 copy-start.1
  526.3 3.1 copy-start.1
  539.3 3.1 copy-start.1
Sparse Core Ops, SparseCore 0:
  31.9 117.5 all-gather.3
  181.9 61.8 reduce-scatter.1
  247.1 101.9 all-gather.5
  352.9 88.8 all-gather.7
